TPU v7x, 256 devices: a whole 4x4x8 slice. The times are simulated.
256 devices in a mesh: dp: 8 (over z_hi, x), expert: 32 (over y, z_lo, core).
Axes of the slice: x: 4, y: 4, z: 8 (z_hi: 2, z_lo: 4; z = z_hi * 4 + z_lo), core: 2. Of those that a mesh axis runs over, the one named last changes fastest.
Arguments:
- tokens: bfloat16 [4096, 3584], P('expert'), may hold values from -6 to 6
- expert_ids: int32 [4096, 8], P('expert'), may hold values from 0 to 31, all different within a row; in each aligned block of 128 rows (0 to 127, 128 to 255, ...) at most 48 rows name the same one
- route_weight: float32 [4096, 8], P('expert'), may hold values from 0.1 to 1
- pair_swap: int32 [16], replicated, may hold values from 0 to 1, as said below
- expert_gate: bfloat16 [32, 3584, 2048], P('expert', None, 'dp'), may hold values from -0.09375 to 0.09375
- expert_up: bfloat16 [32, 3584, 2048], P('expert', None, 'dp'), may hold values from -0.09375 to 0.09375
- expert_down: bfloat16 [32, 2048, 3584], P('expert', 'dp'), may hold values from -0.1875 to 0.1875
- shared_gate: bfloat16 [3584, 2048], P(None, 'dp'), may hold values from -0.09375 to 0.09375
- shared_up: bfloat16 [3584, 2048], P(None, 'dp'), may hold values from -0.09375 to 0.09375
- shared_down: bfloat16 [2048, 3584], P('dp'), may hold values from -0.1875 to 0.1875
Outputs:
- layer_out: bfloat16 [4096, 3584], P('expert', 'dp')
Inputs may be any that keep to these rules, and one draw needn't show every extreme that they name: `expert_ids`: each row names 8 different experts; within the rows of one device (aligned blocks of 128 rows) no expert is named more than 48 times, a bound that some block reaches. `pair_swap`: entry 0 is always 1; the other entries are 0 or 1.
All inputs are finite; a program needn't handle non-finite values.
Results may differ from a plain program's by a relative error of at most 0.012.
Values may be sent and summed in bfloat16 or wider, within the bound.
A program may use at most 192 MiB of HBM per device.

v0:
```python
import jax
import jax.numpy as jnp
from jax import lax
from jax.sharding import PartitionSpec as P

routed_scale = 2.5


def local(
    tokens,
    expert_ids,
    route_weight,
    pair_swap,
    expert_gate,
    expert_up,
    expert_down,
    shared_gate,
    shared_up,
    shared_down,
):
    f32 = jnp.float32
    rows = tokens.shape[0]
    experts = lax.axis_size("expert")
    half = experts // 2
    columns = jnp.arange(experts, dtype=jnp.int32)
    swap = jnp.concatenate([pair_swap, pair_swap])
    stored = jnp.where(swap == 1, (columns + half) % experts, columns)
    mix = route_weight / jnp.sum(route_weight, axis=1, keepdims=True)
    dense = jnp.sum(
        jnp.where(
            expert_ids[:, :, None] == stored[None, None, :], routed_scale * mix[:, :, None], 0.0
        ),
        axis=1,
    )
    every = lax.all_gather(tokens, "expert", axis=0, tiled=True)
    mine = lax.all_to_all(dense, "expert", split_axis=1, concat_axis=0, tiled=True)
    gate_val = jnp.dot(every, expert_gate[0], preferred_element_type=f32)
    up_val = jnp.dot(every, expert_up[0], preferred_element_type=f32)
    act = (jax.nn.silu(gate_val) * up_val * mine).astype(jnp.bfloat16)
    part = jnp.dot(act, expert_down[0], preferred_element_type=f32)
    shared_gv = jnp.dot(tokens, shared_gate, preferred_element_type=f32)
    shared_uv = jnp.dot(tokens, shared_up, preferred_element_type=f32)
    shared_act = (jax.nn.silu(shared_gv) * shared_uv).astype(jnp.bfloat16)
    shared_out = jnp.dot(shared_act, shared_down, preferred_element_type=f32)
    first = lax.psum_scatter(part.astype(jnp.bfloat16), "dp", scatter_dimension=1, tiled=True)
    second = lax.psum_scatter(first, "expert", scatter_dimension=0, tiled=True)
    shared_sum = lax.psum_scatter(
        shared_out.astype(jnp.bfloat16), "dp", scatter_dimension=1, tiled=True
    )
    return (second.astype(f32) + shared_sum.astype(f32)).astype(jnp.bfloat16)


def solution(mesh):
    in_specs = (
        P("expert", None),
        P("expert", None),
        P("expert", None),
        P(),
        P("expert", None, "dp"),
        P("expert", None, "dp"),
        P("expert", "dp", None),
        P(None, "dp"),
        P(None, "dp"),
        P("dp", None),
    )
    return jax.shard_map(
        local, mesh=mesh, in_specs=in_specs, out_specs=P("expert", "dp"), check_vma=False
    )
```

profile of v0, /device:TPU:8, one launch (start us, length us, event | category | flops | bytes accessed | tf_op | source)
XLA Modules:
  0.0 980.6 jit_solution(4599210068851855276)
XLA Ops:
  6.5 0.0 copy-start
  6.5 0.0 all-gather.2.cloned.1.call-start
  6.5 0.7 all-gather.2.cloned.1.call-update
  7.3 0.7 reduce_sum.18
  8.0 0.8 compare_select_fusion.2
  8.8 0.7 divide_multiply_fusion
  9.5 1.4 select_reduce_fusion
  10.8 9.1 all-to-all-start
  20.0 0.0 reduce-scatter.6.cloned.1.call-start
  20.0 155.0 %all-gather.2.cloned.1.call-done = bf16[4096,3584]{1,0:T(8,128)(2,1)} async-done(((bf16[128,3584]{1,0:T(8,128)(2,1)}), bf16[4096,3584]{1,0:T(8,128)(2,1)}) %all-gather.2.cloned.1.call-update) | async-done | bytes 29360144 | tf_op jit(solution)/shard_map/all_gather | solution.py:35
  175.0 15.2 %fusion.7 = f32[4096,256]{1,0:T(8,128)} fusion(bf16[4096,3584]{1,0:T(8,128)(2,1)} %all-gather.2.cloned.1.call-done, bf16[1,3584,256]{2,1,0:T(8,128)(2,1)} %param.14), kind=kOutput, calls=%fused_computation.9 | convolution fusion | flops 7516192768 | bytes 35389440 | tf_op jit(solution)/shard_map/dot_general | solution.py:37
  190.2 0.0 all-to-all-done
  190.2 0.0 copy-done
  190.2 37.4 %convolution_convert_fusion = bf16[4096,3584]{0,1:T(8,128)(2,1)} fusion(bf16[4096,3584]{1,0:T(8,128)(2,1)} %all-gather.2.cloned.1.call-done, f32[4096,256]{1,0:T(8,128)} %fusion.7, f32[4096]{0:T(1024)S(1)} %bitcast.26, bf16[1,256,3584]{2,1,0:T(8,128)(2,1)S(1)} %copy-done, bf16[1,3584,256]{2,1,0:T(8,128)(2,1)} %param.15), kind=kOutput, calls=%fused_computation | convolution fusion | flops 15054405632 | bytes 66600960 | tf_op jit(solution)/shard_map/dot_general | solution.py:40
  227.6 0.0 reduce-scatter.6.cloned.1.call-update
  227.6 0.0 reduce-scatter.10.cloned.1.call-start
  227.6 482.4 %reduce-scatter.6.cloned.1.call-done = bf16[4096,448]{0,1:T(8,128)(2,1)} async-done(((bf16[4096,3584]{0,1:T(8,128)(2,1)}), bf16[4096,448]{0,1:T(8,128)(2,1)}) %reduce-scatter.6.cloned.1.call-update) | async-done | bytes 3670032 | tf_op jit(solution)/shard_map/reduce_scatter | solution.py:45
  710.0 6.4 copy.20
  716.4 0.0 copy-start.2
  716.4 0.0 reduce-scatter.10.cloned.1.call-update
  716.4 0.0 reduce-scatter.8.cloned.1.call-start
  716.5 1.1 copy-done.2
  717.6 0.6 copy-done.3
  718.2 0.4 fusion.19
  718.6 0.0 copy-start.1
  718.6 4.6 convolution_convert_fusion.1
  723.2 0.0 reduce-scatter.8.cloned.1.call-update
  723.2 142.2 %reduce-scatter.10.cloned.1.call-done = bf16[128,448]{1,0:T(8,128)(2,1)} async-done(((bf16[4096,448]{1,0:T(8,128)(2,1)}), bf16[128,448]{1,0:T(8,128)(2,1)}) %reduce-scatter.10.cloned.1.call-update) | async-done | bytes 114704
  865.5 1.0 copy.21
  866.5 106.0 %reduce-scatter.8.cloned.1.call-done = bf16[128,448]{0,1:T(8,128)(2,1)} async-done(((bf16[128,3584]{0,1:T(8,128)(2,1)}), bf16[128,448]{0,1:T(8,128)(2,1)}) %reduce-scatter.8.cloned.1.call-update) | async-done | bytes 114704 | tf_op jit(solution)/shard_map/reduce_scatter | solution.py:47
  972.5 1.6 add_convert_fusion
  974.1 0.0 copy-done.1
  (1 shorter events, 0.0 us)
Async XLA Ops:
  6.5 183.7 %copy-start = (bf16[1,256,3584]{2,1,0:T(8,128)(2,1)S(1)}, bf16[1,256,3584]{2,1,0:T(8,128)(2,1)}, u32[]{:S(2)}) copy-start(bf16[1,256,3584]{2,1,0:T(8,128)(2,1)} %param.16) | copy-start | bytes 5505028
  6.5 168.5 %all-gather.2.cloned.1.call-start = ((), (), s32[]{:S(2)}) async-start(), calls=%async_computation.4 | async-start | bytes 30277632 | tf_op jit(solution)/shard_map/all_gather | solution.py:35
  10.8 179.3 %all-to-all-start = ((f32[128,32,1]{0,2,1:T(1,128)}), f32[128,32,1]{0,2,1:T(1,128)S(1)}, u32[]{:S(2)}, u32[]{:S(2)}) async-start(f32[128,32,1]{0,2,1:T(1,128)} %bitcast.3), calls=%async_computation | async-start | bytes 32768 | tf_op jit(solution)/shard_map/all_to_all | solution.py:36
  20.0 690.0 %reduce-scatter.6.cloned.1.call-start = ((), (), s32[]{:S(2)}) async-start(), calls=%async_computation.5 | async-start | bytes 33030144 | tf_op jit(solution)/shard_map/reduce_scatter | solution.py:45
  227.6 637.9 %reduce-scatter.10.cloned.1.call-start = ((), (), s32[]{:S(2)}) async-start(), calls=%async_computation.7 | async-start | bytes 4325376
  716.4 1.2 copy-start.2
  716.4 1.8 copy-start.3
  716.4 256.1 %reduce-scatter.8.cloned.1.call-start = ((), (), s32[]{:S(2)}) async-start(), calls=%async_computation.6 | async-start | bytes 1032192 | tf_op jit(solution)/shard_map/reduce_scatter | solution.py:47
  718.6 255.5 %copy-start.1 = (bf16[1,256,3584]{2,1,0:T(8,128)(2,1)S(1)}, bf16[1,256,3584]{2,1,0:T(8,128)(2,1)}, u32[]{:S(2)}) copy-start(bf16[1,256,3584]{2,1,0:T(8,128)(2,1)} %param.16) | copy-start | bytes 5505028
Sparse Core Ops, SparseCore 0:
  9.2 165.7 all-gather.1
  227.7 482.2 reduce-scatter.5
  716.6 148.8 reduce-scatter.9
  869.8 102.6 reduce-scatter.7
where the time goes:
time: 981 us
  waiting for transfers between devices  886 us (90%)
  matrix products  57.5 us (6%)
  between operations  13.2 us (1%)
    reduce_scatter x1, waiting for transfers between devices, local(): lax.psum_scatter(part.astype(jnp.bfloat16), 'dp', scatter_dimension=1, ti...  482 us
    all_gather x1, waiting for transfers between devices, local(): every = lax.all_gather(tokens, 'expert', axis=0, tiled=True)  155 us
    unnamed x5, waiting for transfers between devices  143 us
    reduce_scatter x1, waiting for transfers between devices, local(): lax.psum_scatter(shared_out.astype(jnp.bfloat16), 'dp', scatter_dimension...  106 us
    dot_general x1, matrix products, local(): part = jnp.dot(act, expert_down[0], preferred_element_type=f32)  37.4 us
  transfers between devices with their start and end apart: 5, of which 4 were waited for; matrix products, arithmetic and copies ran while one was open for 3% of the time, Pallas kernels for 0%

commit v1 on v0

--- a/solution.py
+++ b/solution.py
@@ -4,6 +4,13 @@
 from jax.sharding import PartitionSpec as P
 
 routed_scale = 2.5
+
+
+def all_by_exchange(array, name, dim):
+    size = lax.axis_size(name)
+    pieces = jnp.stack([array for _ in range(size)])
+    pieces = lax.all_to_all(pieces, name, split_axis=0, concat_axis=0)
+    return jnp.concatenate(pieces, axis=dim)
 
 
 def local(
@@ -32,7 +39,7 @@
         ),
         axis=1,
     )
-    every = lax.all_gather(tokens, "expert", axis=0, tiled=True)
+    every = all_by_exchange(tokens, "expert", 0)
     mine = lax.all_to_all(dense, "expert", split_axis=1, concat_axis=0, tiled=True)
     gate_val = jnp.dot(every, expert_gate[0], preferred_element_type=f32)
     up_val = jnp.dot(every, expert_up[0], preferred_element_type=f32)

time: 981 us -> 1470 us (1.50)
  waiting for transfers between devices: 886 us -> 1360 us
    all_to_all x0 -> x1, waiting for transfers between devices: none -> 632 us  [all_by_exchange(): pieces = lax.all_to_all(pieces, name, split_axis=0, concat_axis=0)]
    all_gather x1 -> x0, waiting for transfers between devices: 155 us -> none  [local(): every = lax.all_gather(tokens, 'expert', axis=0, tiled=True)]
    unnamed x5 -> x4, waiting for transfers between devices: 143 us -> 143 us
  transfers between devices with their start and end apart: 5 -> 5, of which waited for: 4 -> 4; matrix products, arithmetic and copies ran while one was open for 3% -> 1% of each run, Pallas kernels for 0% -> 0%
where the time goes in v1:
time: 1470 us
  waiting for transfers between devices  1360 us (93%)
  matrix products  57.6 us (4%)
  local copies, waits for them, and re-layouts  20 us (1%)
  starting transfers between devices  15.3 us (1%)
    all_to_all x1, waiting for transfers between devices, all_by_exchange(): pieces = lax.all_to_all(pieces, name, split_axis=0, concat_axis=0)  632 us
    reduce_scatter x1, waiting for transfers between devices, local(): lax.psum_scatter(part.astype(jnp.bfloat16), 'dp', scatter_dimension=1, ti...  480 us
    unnamed x4, waiting for transfers between devices  143 us
    reduce_scatter x1, waiting for transfers between devices, local(): lax.psum_scatter(shared_out.astype(jnp.bfloat16), 'dp', scatter_dimension...  105 us
    dot_general x1, matrix products, local(): part = jnp.dot(act, expert_down[0], preferred_element_type=f32)  37.4 us
  transfers between devices with their start and end apart: 5, of which 4 were waited for; matrix products, arithmetic and copies ran while one was open for 1% of the time, Pallas kernels for 0%

profile of v1, /device:TPU:8, one launch (start us, length us, event | category | flops | bytes accessed | tf_op | source)
XLA Modules:
  0.0 1469.0 jit_solution(14508277128556993699)
XLA Ops:
  6.5 0.0 copy-start
  6.5 10.8 stack.2
  17.3 0.0 copy-start.5
  17.4 9.3 all-to-all-start
  26.7 0.0 copy-done.4
  26.7 0.0 copy-done.6
  26.7 0.1 compare_select_fusion.2
  26.8 0.0 copy-done.5
  26.8 0.7 select_reduce_fusion
  27.5 631.9 %all-to-all-done = bf16[32,128,3584]{2,1,0:T(8,128)(2,1)} async-done(((bf16[32,128,3584]{2,1,0:T(8,128)(2,1)}), bf16[32,128,3584]{2,1,0:T(8,128)(2,1)}, u32[]{:S(2)}, u32[]{:S(2)}) %all-to-all-start) | async-done | bytes 29360160 | tf_op jit(solution)/shard_map/all_to_all | solution.py:12
  659.4 5.9 all-to-all-start.1
  665.3 0.0 reduce-scatter.6.cloned.1.call-start
  665.3 15.2 %fusion.7 = f32[4096,256]{1,0:T(8,128)} fusion(bf16[4096,3584]{1,0:T(8,128)(2,1)} %bitcast, bf16[1,3584,256]{2,1,0:T(8,128)(2,1)} %param.14), kind=kOutput, calls=%fused_computation.9 | convolution fusion | flops 7516192768 | bytes 35389440 | tf_op jit(solution)/shard_map/dot_general | solution.py:44
  680.5 0.0 all-to-all-done.1
  680.5 0.0 copy-done
  680.5 37.4 %convolution_convert_fusion = bf16[4096,3584]{0,1:T(8,128)(2,1)} fusion(bf16[4096,3584]{1,0:T(8,128)(2,1)} %bitcast, f32[4096,256]{1,0:T(8,128)} %fusion.7, f32[4096]{0:T(1024)S(1)} %bitcast.27, bf16[1,256,3584]{2,1,0:T(8,128)(2,1)S(1)} %copy-done, bf16[1,3584,256]{2,1,0:T(8,128)(2,1)} %param.15), kind=kOutput, calls=%fused_computation | convolution fusion | flops 15054405632 | bytes 66600960 | tf_op jit(solution)/shard_map/dot_general | solution.py:47
  717.9 0.0 reduce-scatter.6.cloned.1.call-update
  717.9 0.0 reduce-scatter.10.cloned.1.call-start
  718.0 480.3 %reduce-scatter.6.cloned.1.call-done = bf16[4096,448]{0,1:T(8,128)(2,1)} async-done(((bf16[4096,3584]{0,1:T(8,128)(2,1)}), bf16[4096,448]{0,1:T(8,128)(2,1)}) %reduce-scatter.6.cloned.1.call-update) | async-done | bytes 3670032 | tf_op jit(solution)/shard_map/reduce_scatter | solution.py:52
  1198.3 6.4 copy.20
  1204.7 0.0 reduce-scatter.10.cloned.1.call-update
  1204.7 0.0 reduce-scatter.8.cloned.1.call-start
  1204.8 1.1 copy-done.2
  1205.9 0.6 copy-done.3
  1206.5 0.4 fusion.19
  1206.9 0.0 copy-start.1
  1206.9 4.6 convolution_convert_fusion.1
  1211.5 0.0 reduce-scatter.8.cloned.1.call-update
  1211.5 142.9 %reduce-scatter.10.cloned.1.call-done = bf16[128,448]{1,0:T(8,128)(2,1)} async-done(((bf16[4096,448]{1,0:T(8,128)(2,1)}), bf16[128,448]{1,0:T(8,128)(2,1)}) %reduce-scatter.10.cloned.1.call-update) | async-done | bytes 114704
  1354.4 1.0 copy.21
  1355.4 105.4 %reduce-scatter.8.cloned.1.call-done = bf16[128,448]{0,1:T(8,128)(2,1)} async-done(((bf16[128,3584]{0,1:T(8,128)(2,1)}), bf16[128,448]{0,1:T(8,128)(2,1)}) %reduce-scatter.8.cloned.1.call-update) | async-done | bytes 114704 | tf_op jit(solution)/shard_map/reduce_scatter | solution.py:54
  1460.9 1.6 add_convert_fusion
  (7 shorter events, 0.0 us)
Async XLA Ops:
  6.5 674.0 %copy-start = (bf16[1,256,3584]{2,1,0:T(8,128)(2,1)S(1)}, bf16[1,256,3584]{2,1,0:T(8,128)(2,1)}, u32[]{:S(2)}) copy-start(bf16[1,256,3584]{2,1,0:T(8,128)(2,1)} %param.16) | copy-start | bytes 5505028
  17.3 9.4 copy-start.4
  17.3 9.4 copy-start.6
  17.3 9.5 copy-start.5
  17.4 642.0 %all-to-all-start = ((bf16[32,128,3584]{2,1,0:T(8,128)(2,1)}), bf16[32,128,3584]{2,1,0:T(8,128)(2,1)}, u32[]{:S(2)}, u32[]{:S(2)}) async-start(bf16[32,128,3584]{2,1,0:T(8,128)(2,1)} %stack.2), calls=%async_computation | async-start | bytes 58720256 | tf_op jit(solution)/shard_map/all_to_all | solution.py:12
  659.4 21.1 %all-to-all-start.1 = ((f32[128,32,1]{0,2,1:T(1,128)}), f32[128,32,1]{0,2,1:T(1,128)S(1)}, u32[]{:S(2)}, u32[]{:S(2)}) async-start(f32[128,32,1]{0,2,1:T(1,128)} %bitcast.4), calls=%async_computation.1 | async-start | bytes 32768 | tf_op jit(solution)/shard_map/all_to_all | solution.py:43
  665.3 533.0 %reduce-scatter.6.cloned.1.call-start = ((), (), s32[]{:S(2)}) async-start(), calls=%async_computation.5 | async-start | bytes 33030144 | tf_op jit(solution)/shard_map/reduce_scatter | solution.py:52
  717.9 636.4 %reduce-scatter.10.cloned.1.call-start = ((), (), s32[]{:S(2)}) async-start(), calls=%async_computation.7 | async-start | bytes 4325376
  1204.7 1.2 copy-start.2
  1204.7 1.8 copy-start.3
  1204.7 256.1 %reduce-scatter.8.cloned.1.call-start = ((), (), s32[]{:S(2)}) async-start(), calls=%async_computation.6 | async-start | bytes 1032192 | tf_op jit(solution)/shard_map/reduce_scatter | solution.py:54
  1206.9 255.5 %copy-start.1 = (bf16[1,256,3584]{2,1,0:T(8,128)(2,1)S(1)}, bf16[1,256,3584]{2,1,0:T(8,128)(2,1)}, u32[]{:S(2)}) copy-start(bf16[1,256,3584]{2,1,0:T(8,128)(2,1)} %param.16) | copy-start | bytes 5505028
Sparse Core Ops, SparseCore 0:
  718.1 480.1 reduce-scatter.5
  1204.8 149.4 reduce-scatter.9
  1358.8 101.9 reduce-scatter.7
